TPU v7x, 128 devices: a whole 4x4x4 slice. The times are simulated.
128 devices in a mesh: section: 4 (over z), dp: 32 (over y, x, core).
Axes of the slice: x: 4, y: 4, z: 4, core: 2. Of those that a mesh axis runs over, the one named last changes fastest.
Arguments:
- hidden: bfloat16 [64, 4, 8192], P('dp')
- delta: float32 [64, 8192], P('dp'), may hold values from -12 to 12
- gain: float32 [8192], replicated, may hold values from 0.5 to 1.5
- head: bfloat16 [131072, 8192], P(('section', 'dp'))
- targets: int32 [64, 3], replicated, may hold values from 0 to 131071
- tlen: int32 [64], replicated, may hold values from 1 to 3, as said below
Outputs:
- edit_loss: float32 [64], P('dp')
- value_step: float32 [64, 8192], P('dp')
Inputs may be any that keep to these rules, and one draw needn't show every extreme that they name: Entries of targets at positions tlen or later are not read.
All inputs are finite; a program needn't handle non-finite values.
Results may differ from a plain program's by a relative error of at most 0.0003.
The roundings to bfloat16 on the way count: a program that leaves them out, or rounds other values in their place, can miss the bound.
Values may be sent and summed in bfloat16 or wider, within the bound.
A program may use at most 128 MiB of HBM per device.

v0:
```python
import jax
import jax.numpy as jnp
from jax import lax
from jax.sharding import PartitionSpec as P

TGT = 3


EPS = 1e-05
KL_WEIGHT = 0.0625
STEP_RATE = 10.0


def joined(value, axis, join):
    pieces = jax.tree.map(lambda part: lax.all_gather(part, axis), value)
    head = jax.tree.map(lambda part: part[0], pieces)
    tail = jax.tree.map(lambda part: part[1:], pieces)
    running, _ = lax.scan(lambda running, share: (join(running, share), None), head, tail)
    return running


def normalize(values, gain):
    inv = lax.rsqrt(jnp.mean(values * values, axis=-1, keepdims=True) + EPS)
    return (values * inv * gain, inv)


def combine_pair(first, second):
    top = jnp.maximum(first[0], second[0])
    return (top, first[1] * jnp.exp(first[0] - top) + second[1] * jnp.exp(second[0] - top))


def local(hidden, delta, gain, head, targets, tlen):
    edit_dev, slots, width = hidden.shape
    voc_dev = head.shape[0]
    edits = targets.shape[0]
    hid = hidden.astype(jnp.float32)
    shifted = hid + delta[:, None, :]
    normed, inv = normalize(shifted, gain)
    base, unused = normalize(hid[:, slots - 1, :], gain)
    rows = jnp.concatenate(
        [normed.astype(jnp.bfloat16), base.astype(jnp.bfloat16)[:, None, :]], axis=1
    )
    logits = lax.dot_general(
        lax.all_gather(rows, "dp", axis=0, tiled=True),
        head,
        (((2,), (1,)), ((), ())),
        preferred_element_type=jnp.float32,
    )
    local_top = jnp.max(logits, axis=-1)
    local_total = jnp.sum(jnp.exp(logits - local_top[:, :, None]), axis=-1)
    vocab_ids = lax.axis_index(("section", "dp")) * voc_dev + jnp.arange(voc_dev, dtype=jnp.int32)
    hit = targets[:, :, None] == vocab_ids[None, None, :]
    tgt_local = jnp.sum(jnp.where(hit, logits[:, :TGT, :], 0.0), axis=-1)
    top, total = joined((local_top, local_total), ("section", "dp"), combine_pair)
    logz = top + jnp.log(total)
    logp = logits - logz[:, :, None]
    kl_local = jnp.sum(
        jnp.exp(logp[:, TGT + 1, :]) * (logp[:, TGT + 1, :] - logp[:, TGT, :]), axis=-1
    )
    tgt_sum, kl = lax.psum((tgt_local, kl_local), ("section", "dp"))
    tgt_logp = tgt_sum - logz[:, :TGT]
    lengths = tlen.astype(jnp.float32)
    weight = (jnp.arange(TGT, dtype=jnp.int32)[None, :] < tlen[:, None]).astype(
        jnp.float32
    ) / lengths[:, None]
    nll = -jnp.sum(tgt_logp * weight, axis=1)
    loss_all = nll + KL_WEIGHT * kl
    offset = lax.axis_index("dp") * edit_dev
    edit_loss = lax.dynamic_slice_in_dim(loss_all, offset, edit_dev, 0)
    probs = jnp.exp(logp[:, : TGT + 1, :])
    base_prob = jnp.exp(logp[:, TGT + 1, :])
    d_target = (probs[:, :TGT, :] - hit.astype(jnp.float32)) * weight[:, :, None]
    d_kl = KL_WEIGHT * (probs[:, TGT, :] - base_prob)
    dlogits = jnp.concatenate([d_target, d_kl[:, None, :]], axis=1).astype(jnp.bfloat16)
    dlogits = dlogits.reshape(edits * slots, voc_dev)
    own_rows = edit_dev * slots
    full = lax.psum(jnp.dot(dlogits, head, preferred_element_type=jnp.float32), ("section", "dp"))
    mine = lax.dynamic_slice_in_dim(full, offset * slots, own_rows, 0)
    gnorm = mine.reshape(edit_dev, slots, width)
    scaled = gain * gnorm
    inner = jnp.sum(scaled * shifted, axis=-1, keepdims=True)
    gshift = inv * scaled - shifted * inv * inv * inv * inner / width
    value_step = -STEP_RATE * jnp.sum(gshift, axis=1)
    return (edit_loss, value_step)


def solution(mesh):
    placed = (P("dp", None, None), P("dp", None), P(), P(("section", "dp"), None), P(), P())
    return jax.shard_map(
        local, mesh=mesh, in_specs=placed, out_specs=(P("dp"), P("dp", None)), check_vma=False
    )
```

profile of v0, /device:TPU:1, one launch (start us, length us, event | category | flops | bytes accessed | tf_op | source)
XLA Modules:
  0.0 341.1 jit_solution(8089196825113170265)
XLA Ops:
  7.2 0.0 all-gather.6.cloned.1.call-start
  7.2 0.9 convert_element_type.28
  8.1 1.1 multiply_reduce_fusion
  9.2 0.2 multiply_reduce_fusion.1
  9.4 1.1 multiply_convert_fusion
  10.5 0.9 multiply_convert_fusion.1
  11.4 0.8 pad_maximum_fusion.1
  12.2 0.0 all-gather.6.cloned.1.call-update
  12.3 0.0 all-reduce.3.cloned.1.call-start
  12.3 0.7 convert_element_type.32
  13.0 0.7 convert_divide_fusion
  13.7 55.0 %all-gather.6.cloned.1.call-done = bf16[64,5,8192]{2,1,0:T(8,128)(2,1)} async-done(((bf16[2,5,8192]{2,1,0:T(8,128)(2,1)}), bf16[64,5,8192]{2,1,0:T(8,128)(2,1)}) %all-gather.6.cloned.1.call-update) | async-done | bytes 5242896 | tf_op jit(solution)/shard_map/all_gather | solution.py:44
  68.7 15.8 %fusion.22 = (f32[64,5]{0,1:T(8,128)S(1)}, f32[64,5,1024]{2,0,1:T(8,128)S(1)}) fusion(bf16[1024,8192]{1,0:T(8,128)(2,1)} %param.11, bf16[64,5,8192]{2,1,0:T(8,128)(2,1)} %all-gather.6.cloned.1.call-done), kind=kOutput, calls=%fused_computation.52 | convolution fusion | flops 5369036288 | bytes 23332096 | tf_op jit(solution)/shard_map/dot_general | solution.py:43
  84.5 0.0 copy-start.3
  84.5 0.3 exponential_reduce_fusion
  84.8 36.5 %all-gather.3 = f32[128,64,5]{1,2,0:T(8,128)S(1)} all-gather(f32[1,64,5]{1,2,0:T(8,128)S(1)} %bitcast.28), channel_id=3, replica_groups=mesh['section'=4,'dp'=32] {'section','dp'}, dimensions={0}, use_global_device_ids=true | all-gather | bytes 165120 | tf_op jit(solution)/shard_map/all_gather | solution.py:15
  121.3 34.2 %all-gather.2 = f32[128,64,5]{1,2,0:T(8,128)S(1)} all-gather(f32[1,64,5]{1,2,0:T(8,128)S(1)} %bitcast.27), channel_id=2, replica_groups=mesh['section'=4,'dp'=32] {'section','dp'}, dimensions={0}, use_global_device_ids=true | all-gather | bytes 165120 | tf_op jit(solution)/shard_map/all_gather | solution.py:15
  155.6 4.5 %while.12 = (s32[]{:T(128)}, f32[64,5]{0,1:T(8,128)S(1)}, f32[64,5]{0,1:T(8,128)S(1)}, f32[127,64,5]{1,2,0:T(8,128)S(1)}, f32[127,64,5]{1,2,0:T(8,128)S(1)}, /*index=5*/s32[]{:T(128)}) while((s32[]{:T(128)}, f32[64,5]{0,1:T(8,128)S(1)}, f32[64,5]{0,1:T(8,128)S(1)}, f32[127,64,5]{1,2,0:T(8,128)S(1)}, f32[127,64,5]{1,2,0:T(8,128)S(1)}, ...), condition=%wide.region_7.8_spmd, body=%wide.region_6.7_spmd.sunk | while | flops 1922 | bytes 7761 | solution.py:18
  160.1 0.2 broadcast_subtract_fusion
  160.3 0.1 slice_exponential_fusion
  160.4 0.2 fusion.14
  160.6 0.0 copy-done.3
  160.6 0.4 fusion.12
  161.1 0.4 copy.13
  161.5 0.1 convert_element_type.34
  161.6 12.5 %fusion.24 = f32[256,8192]{1,0:T(8,128)} fusion(bf16[256,1024]{1,0:T(8,128)(2,1)S(1)} %convert_element_type.34, bf16[1024,8192]{1,0:T(8,128)(2,1)} %param.11), kind=kOutput, calls=%fused_computation.54 | convolution fusion | flops 4294967296 | bytes 25690112 | tf_op jit(solution)/shard_map/dot_general | solution.py:77
  174.1 0.0 copy-start.4
  174.1 0.0 copy-start
  174.1 0.0 copy-start.1
  174.1 0.0 copy-start.2
  174.1 0.0 all-reduce.3.cloned.1.call-update
  174.1 62.6 %all-reduce = (f32[64]{0:T(128)S(1)}, f32[64,3]{0,1:T(4,128)S(1)}) all-reduce(f32[64]{0:T(128)S(1)} %get-tuple-element.47, f32[64,3]{0,1:T(4,128)S(1)} %get-tuple-element.49), channel_id=1, replica_groups=mesh['section'=4,'dp'=32] {'section','dp'}, use_global_device_ids=true, to_apply=%region_10.11 | all-reduce | flops 256 | bytes 2048 | tf_op jit(solution)/shard_map/psum | solution.py:60
  236.8 0.0 copy-done.4
  236.8 0.6 dynamic_slice.13
  237.4 94.6 %all-reduce.3.cloned.1.call-done = f32[256,8192]{1,0:T(8,128)} async-done(((f32[256,8192]{1,0:T(8,128)}), f32[256,8192]{1,0:T(8,128)}) %all-reduce.3.cloned.1.call-update) | async-done | bytes 8388624 | tf_op jit(solution)/shard_map/psum | solution.py:77
  332.0 1.0 constant_dynamic-slice_fusion
  333.0 0.1 reshape.88
  333.0 0.0 copy-done
  333.1 0.0 copy-done.1
  333.1 0.0 copy-done.2
  333.1 0.5 fusion.23
  333.6 0.7 broadcast_multiply_fusion
  (138 shorter events, 2.2 us)
Async XLA Ops:
  7.2 61.5 %all-gather.6.cloned.1.call-start = ((), (), s32[]{:S(2)}) async-start(), calls=%async_computation | async-start | bytes 8650752 | tf_op jit(solution)/shard_map/all_gather | solution.py:44
  12.3 319.7 %all-reduce.3.cloned.1.call-start = ((), (), s32[]{:S(2)}) async-start(), calls=%async_computation.1 | async-start | bytes 16777216 | tf_op jit(solution)/shard_map/psum | solution.py:77
  84.5 76.1 %copy-start.3 = (s32[64,3]{0,1:T(4,128)S(1)}, s32[64,3]{0,1:T(4,128)}, u32[]{:S(2)}) copy-start(s32[64,3]{0,1:T(4,128)} %param.12) | copy-start | bytes 2308
  174.1 62.7 %copy-start.4 = (s32[64]{0:T(128)S(1)}, s32[64]{0:T(128)}, u32[]{:S(2)}) copy-start(s32[64]{0:T(128)} %param.13) | copy-start | bytes 772
  174.1 159.0 %copy-start = (bf16[2,4,8192]{2,1,0:T(4,128)(2,1)S(1)}, bf16[2,4,8192]{2,1,0:T(4,128)(2,1)}, u32[]{:S(2)}) copy-start(bf16[2,4,8192]{2,1,0:T(4,128)(2,1)} %param.8) | copy-start | bytes 393220
  174.1 159.0 %copy-start.1 = (f32[2,8192]{1,0:T(2,128)S(1)}, f32[2,8192]{1,0:T(2,128)}, u32[]{:S(2)}) copy-start(f32[2,8192]{1,0:T(2,128)} %param.9) | copy-start | bytes 196612
  174.1 159.0 %copy-start.2 = (f32[8192]{0:T(1024)S(1)}, f32[8192]{0:T(1024)}, u32[]{:S(2)}) copy-start(f32[8192]{0:T(1024)} %param.10) | copy-start | bytes 98308
Sparse Core Ops, SparseCore 0:
  12.4 56.2 all-gather.5
  174.3 157.6 all-reduce.2
where the time goes:
time: 341 us
  waiting for transfers between devices  150 us (44%)
  blocking collectives  133 us (39%)
  matrix products  28.3 us (8%)
  between operations  14.2 us (4%)
  other arithmetic  10.6 us (3%)
    psum x1, waiting for transfers between devices, local(): lax.psum(jnp.dot(dlogits, head, preferred_element_type=jnp.float32), ('se...  94.6 us
    all_gather x2, blocking collectives, joined(): pieces = jax.tree.map(lambda part: lax.all_gather(part, axis), value)  70.7 us
    psum x1, blocking collectives, local(): tgt_sum, kl = lax.psum((tgt_local, kl_local), ('section', 'dp'))  62.6 us
    all_gather x1, waiting for transfers between devices, local(): lax.all_gather(rows, 'dp', axis=0, tiled=True)  55 us
    dot_general x1, matrix products, local(): lax.dot_general(lax.all_gather(rows, 'dp', axis=0, tiled=True), head, (((...  15.8 us
    dot_general x1, matrix products, local(): jnp.dot(dlogits, head, preferred_element_type=jnp.float32)  12.5 us
  transfers between devices with their start and end apart: 2, of which 2 were waited for; matrix products, arithmetic and copies ran while one was open for 1% of the time, Pallas kernels for 0%

commit v1 on v0

v1 whole, which is shorter than its diff:
```python
import jax
import jax.numpy as jnp
from jax import lax
from jax.sharding import PartitionSpec as P

TGT = 3


EPS = 1e-05
KL_WEIGHT = 0.0625
STEP_RATE = 10.0


def normalize(values, gain):
    inv = lax.rsqrt(jnp.mean(values * values, axis=-1, keepdims=True) + EPS)
    return (values * inv * gain, inv)


def local(hidden, delta, gain, head, targets, tlen):
    edit_dev, slots, width = hidden.shape
    voc_dev = head.shape[0]
    edits = targets.shape[0]
    every = ("section", "dp")
    hid = hidden.astype(jnp.float32)
    shifted = hid + delta[:, None, :]
    normed, inv = normalize(shifted, gain)
    base, unused = normalize(hid[:, slots - 1, :], gain)
    rows = jnp.concatenate(
        [normed.astype(jnp.bfloat16), base.astype(jnp.bfloat16)[:, None, :]], axis=1
    )
    logits = lax.dot_general(
        lax.all_gather(rows, "dp", axis=0, tiled=True),
        head,
        (((2,), (1,)), ((), ())),
        preferred_element_type=jnp.float32,
    )
    local_top = jnp.max(logits, axis=-1)
    local_exp = jnp.exp(logits - local_top[:, :, None])
    local_total = jnp.sum(local_exp, axis=-1)
    gap = jnp.sum(
        local_exp[:, TGT + 1, :] * (logits[:, TGT + 1, :] - logits[:, TGT, :]), axis=-1
    )
    vocab_ids = lax.axis_index(every) * voc_dev + jnp.arange(voc_dev, dtype=jnp.int32)
    hit = targets[:, :, None] == vocab_ids[None, None, :]
    tgt_local = jnp.sum(jnp.where(hit, logits[:, :TGT, :], 0.0), axis=-1)
    packed = jnp.concatenate(
        [
            local_top.reshape(-1),
            local_total.reshape(-1),
            gap,
            tgt_local.reshape(-1),
            inv.reshape(-1),
        ]
    )
    every_stat = lax.all_gather(packed, every)
    n = edits * (TGT + 2)
    tops = every_stat[:, :n].reshape(-1, edits, TGT + 2)
    top = jnp.max(tops, axis=0)
    factor = jnp.exp(tops - top[None])
    total = jnp.sum(every_stat[:, n : 2 * n].reshape(-1, edits, TGT + 2) * factor, axis=0)
    gap_all = jnp.sum(every_stat[:, 2 * n : 2 * n + edits] * factor[:, :, TGT + 1], axis=0)
    first = 2 * n + edits
    tgt_sum = jnp.sum(every_stat[:, first : first + edits * TGT], axis=0).reshape(edits, TGT)
    dp = lax.axis_size("dp")
    inv_all = every_stat[:dp, first + edits * TGT :].reshape(edits, slots)
    logz = top + jnp.log(total)
    kl = gap_all / total[:, TGT + 1] - logz[:, TGT + 1] + logz[:, TGT]
    logp = logits - logz[:, :, None]
    tgt_logp = tgt_sum - logz[:, :TGT]
    lengths = tlen.astype(jnp.float32)
    weight = (jnp.arange(TGT, dtype=jnp.int32)[None, :] < tlen[:, None]).astype(
        jnp.float32
    ) / lengths[:, None]
    nll = -jnp.sum(tgt_logp * weight, axis=1)
    loss_all = nll + KL_WEIGHT * kl
    offset = lax.axis_index("dp") * edit_dev
    edit_loss = lax.dynamic_slice_in_dim(loss_all, offset, edit_dev, 0)
    probs = jnp.exp(logp)
    d_target = (probs[:, :TGT, :] - hit.astype(jnp.float32)) * weight[:, :, None]
    d_kl = KL_WEIGHT * (probs[:, TGT, :] - probs[:, TGT + 1, :])
    dlogits = jnp.concatenate([d_target, d_kl[:, None, :]], axis=1).astype(jnp.bfloat16)
    inner_local = jnp.sum(dlogits.astype(jnp.float32) * logits[:, :slots, :], axis=-1)
    gnorm = jnp.einsum("esv,vd->sed", dlogits, head, preferred_element_type=jnp.float32)
    mixed = jnp.sum(gnorm * inv_all.T[:, :, None], axis=0)
    full, inner = lax.psum((mixed, inner_local), every)
    mine = lax.dynamic_slice_in_dim(full, offset, edit_dev, 0)
    mine_inner = lax.dynamic_slice_in_dim(inner, offset, edit_dev, 0)[:, :, None]
    back = jnp.sum(shifted * (inv * inv * mine_inner / width), axis=1)
    value_step = -STEP_RATE * (gain * mine - back)
    return (edit_loss, value_step)


def solution(mesh):
    placed = (P("dp", None, None), P("dp", None), P(), P(("section", "dp"), None), P(), P())
    return jax.shard_map(
        local, mesh=mesh, in_specs=placed, out_specs=(P("dp"), P("dp", None)), check_vma=False
    )
```

time: 341 us -> 409 us (1.20)
  waiting for transfers between devices: 150 us -> 284 us
  blocking collectives: 133 us -> 63.7 us
  local copies, waits for them, and re-layouts: 2.39 us -> 7.68 us
    unnamed x2 -> x4, waiting for transfers between devices: 0.03 us -> 145 us
    all_gather x2 -> x0, blocking collectives: 70.7 us -> none  [joined(): pieces = jax.tree.map(lambda part: lax.all_gather(part, axis), value)]
    psum x1, waiting for transfers between devices: 94.6 us -> 82 us  [local(): full, inner = lax.psum((mixed, inner_local), every)]
  transfers between devices with their start and end apart: 2 -> 3, of which waited for: 2 -> 3; matrix products, arithmetic and copies ran while one was open for 1% -> 0% of each run, Pallas kernels for 0% -> 0%
where the time goes in v1:
time: 409 us; the launch traced here: 408 us
  waiting for transfers between devices  284 us (69%)
  blocking collectives  63.7 us (16%)
  matrix products  27.6 us (7%)
  between operations  14 us (3%)
  other arithmetic  11.4 us (3%)
  local copies, waits for them, and re-layouts  7.68 us (2%)
    unnamed x4, waiting for transfers between devices  145 us
    psum x1, waiting for transfers between devices, local(): full, inner = lax.psum((mixed, inner_local), every)  82 us
    psum x1, blocking collectives, local(): full, inner = lax.psum((mixed, inner_local), every)  63.7 us
    all_gather x1, waiting for transfers between devices, local(): lax.all_gather(rows, 'dp', axis=0, tiled=True)  56.3 us
    dot_general x1, matrix products, local(): lax.dot_general(lax.all_gather(rows, 'dp', axis=0, tiled=True), head, (((...  15.8 us
    dot_general x1, matrix products, local(): jnp.einsum('esv,vd->sed', dlogits, head, preferred_element_type=jnp.float32)  11.8 us
  transfers between devices with their start and end apart: 3, of which 3 were waited for; matrix products, arithmetic and copies ran while one was open for 0% of the time, Pallas kernels for 0%

profile of v1, /device:TPU:1, one launch (start us, length us, event | category | flops | bytes accessed | tf_op | source)
XLA Modules:
  0.0 408.3 jit_solution(15002139512185290136)
XLA Ops:
  7.2 0.9 convert_element_type.27
  8.1 0.2 multiply_reduce_fusion.2
  8.3 1.1 multiply_reduce_fusion.1
  9.4 0.1 copy.45
  9.5 0.1 copy.32
  9.6 0.9 multiply_convert_fusion.1
  10.5 1.1 multiply_convert_fusion
  11.6 0.8 pad_maximum_fusion.2
  12.6 56.3 %all-gather.3.cloned.1.call-done = bf16[64,5,8192]{2,1,0:T(8,128)(2,1)} async-done(((bf16[2,5,8192]{2,1,0:T(8,128)(2,1)}), bf16[64,5,8192]{2,1,0:T(8,128)(2,1)}) %all-gather.3.cloned.1.call-update) | async-done | bytes 5242896 | tf_op jit(solution)/shard_map/all_gather | solution.py:32
  68.9 15.8 %fusion.30 = (f32[64,5]{0,1:T(8,128)S(1)}, f32[64,5,1024]{2,0,1:T(8,128)S(1)}) fusion(bf16[1024,8192]{1,0:T(8,128)(2,1)} %param.9, bf16[64,5,8192]{2,1,0:T(8,128)(2,1)} %all-gather.3.cloned.1.call-done), kind=kOutput, calls=%fused_computation.55 | convolution fusion | flops 5369036288 | bytes 23332096 | tf_op jit(solution)/shard_map/dot_general | solution.py:31
  84.7 0.1 copy.34
  84.8 0.3 fusion.28
  85.1 0.1 fusion.22
  85.2 0.1 copy.35
  85.3 0.1 reshape.129
  85.5 0.2 fusion.15
  85.7 0.1 copy.36
  85.8 0.1 reshape.130
  86.0 0.1 reshape.128
  86.2 0.3 dynamic-update-slice
  86.5 0.8 copy-done.1
  87.3 0.2 all-reduce.4.cloned.1.call-start
  87.6 145.2 %all-reduce.6.cloned.1.call-done = f32[115712]{0:T(1024)} async-done(((f32[115712]{0:T(1024)}), f32[115712]{0:T(1024)}) %all-reduce.6.cloned.1.call-update) | async-done | bytes 462864
  232.8 1.5 reshape.134
  234.3 0.7 fusion.29
  235.0 0.1 fusion.23
  235.2 0.1 reduce_max.22
  235.3 0.1 slice_reduce_fusion
  235.4 0.1 reduce_sum.117
  235.6 0.3 copy-done.9
  235.9 0.3 copy-done.7
  236.2 0.3 subtract_exponential_fusion
  236.5 0.1 reshape.131
  236.7 0.7 convert_divide_fusion
  237.4 0.7 copy.42
  238.0 0.7 fusion.20
  238.7 0.9 fusion.18
  239.8 11.8 %fusion.11 = f32[64,8192]{1,0:T(8,128)} fusion(f32[4,64]{1,0:T(4,128)S(1)} %copy.43, bf16[1024,8192]{1,0:T(8,128)(2,1)} %param.9, bf16[64,1,1024]{2,0,1:T(8,128)(2,1)} %fusion.20, bf16[64,3,1024]{2,0,1:T(8,128)(2,1)S(1)} %fusion.18), kind=kOutput, calls=%fused_computation.7 | convolution fusion | flops 4298899456 | bytes 19399680 | tf_op jit(solution)/shard_map/esv,vd->sed/dot_general | solution.py:83
  251.7 0.7 copy-done.10
  252.5 0.2 fusion.14
  252.7 63.7 %psum.15 = f32[64,4]{0,1:T(4,128)S(1)} all-reduce(f32[64,4]{0,1:T(4,128)S(1)} %fusion.14), channel_id=1, replica_groups=mesh['section'=4,'dp'=32] {'section','dp'}, use_global_device_ids=true, to_apply=%region_14.15 | all-reduce | flops 256 | bytes 2048 | tf_op jit(solution)/shard_map/psum | solution.py:85
  316.5 0.1 copy.44
  316.7 0.1 copy.38
  317.0 0.2 slice_reduce_fusion.2
  317.3 0.6 dynamic_slice.9
  317.9 0.2 multiply_reduce_fusion
  318.1 82.0 %all-reduce.4.cloned.1.call-done = f32[64,8192]{1,0:T(8,128)} async-done(((f32[64,8192]{1,0:T(8,128)}), f32[64,8192]{1,0:T(8,128)}) %all-reduce.4.cloned.1.call-update) | async-done | bytes 2097168 | tf_op jit(solution)/shard_map/psum | solution.py:85
  400.1 1.6 subtract_multiply_fusion
  (57 shorter events, 1.2 us)
Async XLA Ops:
  7.2 61.7 %all-gather.3.cloned.1.call-start = ((), (), s32[]{:S(2)}) async-start(), calls=%async_computation | async-start | bytes 8650752 | tf_op jit(solution)/shard_map/all_gather | solution.py:32
  9.5 3.1 copy-start.13
  12.5 220.4 %all-reduce.6.cloned.1.call-start = ((), (), s32[]{:S(2)}) async-start(), calls=%async_computation.2 | async-start | bytes 925696
  12.6 72.9 %copy-start.12 = (s32[1024]{0:T(1024)}, s32[1024]{0:T(1024)S(1)}, u32[]{:S(2)}) copy-start(s32[1024]{0:T(1024)S(1)} %iota_add_fusion) | copy-start | bytes 12292
  84.7 0.8 copy-start.15
  84.8 2.8 copy-start.17
  86.5 0.8 copy-start.1
  87.3 312.8 %all-reduce.4.cloned.1.call-start = ((), (), s32[]{:S(2)}) async-start(), calls=%async_computation.1 | async-start | bytes 4194304 | tf_op jit(solution)/shard_map/psum | solution.py:85
  235.3 0.6 copy-start.9
  235.6 0.6 copy-start.7
  236.2 1.9 copy-start.2
  251.6 0.8 copy-start.10
  251.6 0.9 copy-start.6
  251.6 64.8 %copy-start.14 = (f32[2,4]{0,1:T(4,128)S(1)}, f32[2,4]{0,1:T(4,128)}, u32[]{:S(2)}) copy-start(f32[2,4]{0,1:T(4,128)} %copy-done.13) | copy-start | bytes 100
  251.6 65.1 %copy-start.4 = (f32[128,320]{1,0:T(8,128)S(1)}, f32[128,320]{1,0:T(8,128)}, u32[]{:S(2)}) copy-start(f32[128,320]{1,0:T(8,128)} %get-tuple-element.6) | copy-start | bytes 491524
  251.6 65.4 %copy-start.3 = (f32[64,5]{1,0:T(8,128)S(1)}, f32[64,5]{1,0:T(8,128)}, u32[]{:S(2)}) copy-start(f32[64,5]{1,0:T(8,128)} %copy-done.2) | copy-start | bytes 3844
  251.6 65.4 %copy-start.8 = (f32[64,5]{1,0:T(8,128)S(1)}, f32[64,5]{1,0:T(8,128)}, u32[]{:S(2)}) copy-start(f32[64,5]{1,0:T(8,128)} %copy-done.7) | copy-start | bytes 3844
  251.6 65.6 %copy-start.16 = (f32[64]{0:T(128)S(1)}, f32[64]{0:T(128)}, u32[]{:S(2)}) copy-start(f32[64]{0:T(128)} %get-tuple-element.9) | copy-start | bytes 772
  251.6 66.2 %copy-start = (bf16[2,4,8192]{2,1,0:T(4,128)(2,1)S(1)}, bf16[2,4,8192]{2,1,0:T(4,128)(2,1)}, u32[]{:S(2)}) copy-start(bf16[2,4,8192]{2,1,0:T(4,128)(2,1)} %param.6) | copy-start | bytes 393220
  251.6 66.2 %copy-start.5 = (f32[2,8192]{1,0:T(2,128)S(1)}, f32[2,8192]{1,0:T(2,128)}, u32[]{:S(2)}) copy-start(f32[2,8192]{1,0:T(2,128)} %param.7) | copy-start | bytes 196612
  251.7 148.5 %copy-start.11 = (f32[8192]{0:T(1024)S(1)}, f32[8192]{0:T(1024)}, u32[]{:S(2)}) copy-start(f32[8192]{0:T(1024)} %param.8) | copy-start | bytes 98308
Sparse Core Ops, SparseCore 0:
  12.6 56.2 all-gather.2
  87.5 145.3 all-reduce.5
  251.8 148.2 all-reduce.3

commit v2 on v0

v2 whole, which is shorter than its diff:
```python
import functools

import jax
import jax.numpy as jnp
from jax import lax
from jax.experimental import pallas as pl
from jax.experimental.pallas import tpu as pltpu
from jax.sharding import PartitionSpec as P

TGT = 3
EPS = 1e-05
KL_WEIGHT = 0.0625
STEP_RATE = 10.0
MESH = pl.DeviceIdType.MESH
F32 = jnp.float32
BF16 = jnp.bfloat16

D = 8192
V = 1024
EDITS = 64
SLICE = 1024
HALF = 512
TILE = 128
UCOLS = TILE + 4 * SLICE


def kernel(
    hidden, delta, gain, head, targets, tlen, step_out, loss_out,
    hv, rows, acc, dl, a2a_src, a2a_in, asm, stc, str_, st1, st2, st3,
    usend, precv, xrecv, zsrc, zrecv, hsem, ssem, rsem,
):
    z = lax.axis_index("section")
    dp = lax.axis_index("dp")
    y = dp // 8
    x = (dp // 2) % 4
    c = dp % 2
    g = dp % 8
    chip = dp // 2
    u = z * 2 + c

    def dev(zz, yy, xx, cc):
        return (zz, (yy * 4 + xx) * 2 + cc)

    def at(v, k):
        return (v + k) % 4

    count = [0]

    def ids(n=1):
        first = count[0]
        count[0] += n
        return first

    def remote(src, dst, i, device):
        return pltpu.make_async_remote_copy(
            src_ref=src, dst_ref=dst, send_sem=ssem.at[i], recv_sem=rsem.at[i],
            device_id=device, device_id_type=MESH,
        )

    sent = []

    def head_copy(k):
        return pltpu.make_async_copy(
            head.at[:, pl.ds(k * SLICE, SLICE)], hv.at[k], hsem.at[k]
        )

    for k in range(8):
        head_copy(k).start()

    barrier = pltpu.get_barrier_semaphore()
    peers = []
    for j in range(1, 16):
        peers.append(dev(z, at(y, j // 4), at(x, j % 4), c))
    for j in range(4):
        peers.append(dev(z, y, at(x, j), 1 - c))
    for j in range(1, 4):
        peers.append(dev(at(z, j), y, x, c))
        peers.append(dev(at(z, j), y, x, 1 - c))
    for p in peers:
        pl.semaphore_signal(barrier, inc=1, device_id=p, device_id_type=MESH)

    dlt = delta[...]
    gn = gain[...]
    invs = []
    for s in range(5):
        val = hidden[:, min(s, 3), :].astype(F32)
        if s < 4:
            val = val + dlt
        inv = lax.rsqrt(jnp.mean(val * val, axis=-1, keepdims=True) + EPS)
        invs.append(inv)
        out = (val * inv * gn).astype(BF16)
        for k in range(8):
            a2a_src[k, s] = out[:, k * SLICE : (k + 1) * SLICE]

    pl.semaphore_wait(barrier, len(peers))

    base = ids(8)
    a2a = []
    for j in range(1, 8):
        to = (g + j) % 8
        cp = remote(a2a_src.at[to], a2a_in.at[g], base + j, (z, y * 8 + to))
        cp.start()
        a2a.append(cp)
    sent += a2a
    a2a_in[g] = a2a_src[g]
    for cp in a2a:
        cp.wait_recv()
    for s in range(5):
        for k in range(8):
            asm[s, 2 * k : 2 * k + 2, :] = a2a_in[k, s].astype(F32)
    for s in range(5):
        piece = asm[s].astype(BF16)
        rows[c, x, 0, s, y] = piece[:, :HALF]
        rows[c, x, 1, s, y] = piece[:, HALF:]

    LO, HI = pl.ds(0, 256), pl.ds(256, 256)
    XP, XM = dev(z, y, at(x, 1), c), dev(z, y, at(x, 3), c)
    YP, YM = dev(z, at(y, 1), x, c), dev(z, at(y, 3), x, c)
    PART = dev(z, y, x, 1 - c)

    class Ring:
        KEYS = ("+lo", "-hi", "+hi", "-lo", "f+", "f-")

        def __init__(self, block, plus, minus, place):
            self.block, self.plus, self.minus, self.place = block, plus, minus, place
            self.first = ids(6)

        def copy(self, key):
            where = {"f+": 3, "f-": 1}.get(key, 0)
            q = LO if key in ("+lo", "-lo", "f+") else HI
            device = self.plus if key in ("+lo", "+hi", "f+") else self.minus
            ref = self.block(at(self.place, where), q)
            return remote(ref, ref, self.first + self.KEYS.index(key), device)

        def start(self):
            for key in self.KEYS[:4]:
                self.copy(key).start()

        def relay(self):
            self.copy("+lo").wait_recv()
            self.copy("f+").start()
            self.copy("-hi").wait_recv()
            self.copy("f-").start()

        def near(self, which):
            self.copy(which).wait_recv()

        def far(self):
            self.copy("f+").wait_recv()
            self.copy("f-").wait_recv()

        def drain(self):
            for key in self.KEYS:
                self.copy(key).wait_send()

    a1 = Ring(lambda w, q: rows.at[c, x, 0, :, w, :, q], YP, YM, y)
    b1 = Ring(lambda w, q: rows.at[c, w, 1, :, y, :, q], XP, XM, x)
    a2 = Ring(lambda w, q: rows.at[c, w, 0, :, :, :, q], XP, XM, x)
    b2 = {
        k: Ring(lambda w, q, k=k: rows.at[c, at(x, k), 1, :, w, :, q], YP, YM, y)
        for k in range(4)
    }
    pair_ids = ids(8)

    def pair(k, h):
        ref = rows.at[c, at(x, k), h]
        return remote(ref, ref, pair_ids + 2 * k + h, PART)

    def give(k, h):
        pair(k, h).start()

    def take(k, h):
        pair(k, h).wait_recv()

    acc[...] = jnp.zeros_like(acc)
    a1.start()
    b1.start()
    b2[0].start()
    a1.relay()
    b1.relay()
    a1.near("+hi")
    a1.near("-lo")
    a1.far()
    a2.start()
    give(0, 0)
    b1.near("+hi")
    b2[3].start()
    b1.near("-lo")
    b2[1].start()
    for k in range(8):
        head_copy(k).wait()

    def s1():
        b1.far()
        b2[2].start()
        b2[0].relay()
        take(0, 0)

    def s2():
        b2[0].near("+hi")
        b2[0].near("-lo")
        a2.relay()
        b2[0].far()
        give(0, 1)

    def s3():
        b2[3].relay()
        take(0, 1)

    def s4():
        a2.near("+hi")
        give(3, 0)

    def s5():
        a2.near("-lo")
        give(1, 0)
        b2[1].relay()

    def s6():
        take(3, 0)

    def s7():
        take(1, 0)

    def s8():
        b2[2].relay()
        b2[3].near("+hi")
        b2[3].near("-lo")
        b2[3].far()
        give(3, 1)

    def s9():
        b2[1].near("+hi")
        b2[1].near("-lo")
        b2[1].far()
        give(1, 1)

    def s10():
        take(3, 1)

    def s11():
        take(1, 1)

    def s12():
        a2.far()
        give(2, 0)

    def s13():
        b2[2].near("+hi")
        b2[2].near("-lo")
        b2[2].far()
        give(2, 1)

    def s14():
        take(2, 0)

    def s15():
        take(2, 1)

    actions = [None, s1, s2, s3, s4, s5, s6, s7, s8, s9, s10, s11, s12, s13, s14, s15]
    order = [
        (0, 0, 0), (1, 0, 0), (0, 0, 1), (1, 0, 1),
        (0, 3, 0), (0, 1, 0), (1, 3, 0), (1, 1, 0),
        (0, 3, 1), (0, 1, 1), (1, 3, 1), (1, 1, 1),
        (0, 2, 0), (0, 2, 1), (1, 2, 0), (1, 2, 1),
    ]

    def pick(t, values):
        out = t * 0 + values[0]
        for k, v in enumerate(values):
            if k:
                out = jnp.where(t == k, v, out)
        return out

    def step(t, carry):
        for k, act in enumerate(actions):
            if act is not None:
                pl.when(t == k)(act)
        rc = pick(t, [o[0] for o in order])
        rx = pick(t, [o[1] for o in order])
        h = pick(t, [o[2] for o in order])
        cc = (c + rc) % 2
        xx = (x + rx) % 4
        lhs = rows[cc, xx, h].reshape(5 * EDITS, HALF)
        rhs = hv[xx * 2 + cc, :, pl.ds(pl.multiple_of(h * HALF, HALF), HALF)]
        acc[...] += lax.dot_general(
            lhs, rhs, (((1,), (1,)), ((), ())), preferred_element_type=F32
        )
        return carry

    lax.fori_loop(0, 16, step, 0)

    lane = lax.broadcasted_iota(jnp.int32, (EDITS, TILE), 1)
    row = lax.broadcasted_iota(jnp.int32, (EDITS, 1), 0)
    first = (z * 32 + dp) * V
    vocab = first + lax.broadcasted_iota(jnp.int32, (1, V), 1)

    def logits(s):
        return acc[s * EDITS : (s + 1) * EDITS, :]

    stc[5 * EDITS :, :] = jnp.zeros((EDITS, TILE), F32)
    for s in range(5):
        lg = logits(s)
        top = jnp.max(lg, axis=-1, keepdims=True)
        ex = jnp.exp(lg - top)
        tot = jnp.sum(ex, axis=-1, keepdims=True)
        if s < TGT:
            hit = targets[:, s : s + 1] == vocab
            extra = jnp.sum(jnp.where(hit, lg, 0.0), axis=-1, keepdims=True)
        elif s == TGT:
            extra = jnp.zeros((EDITS, 1), F32)
        else:
            extra = jnp.sum(ex * (lg - logits(TGT)), axis=-1, keepdims=True)
        put = jnp.where(lane == 0, top, jnp.where(lane == 1, tot, extra))
        if s < 4:
            iv = invs[s]
            ivc = jnp.where(
                row == 2 * dp, iv[0:1, :], jnp.where(row == 2 * dp + 1, iv[1:2, :], 0.0)
            )
            put = jnp.where(lane == 3, ivc, put)
        stc[s * EDITS : (s + 1) * EDITS, :] = put

    lane3 = lax.broadcasted_iota(jnp.int32, (1, 3 * TILE), 1)
    row8 = lax.broadcasted_iota(jnp.int32, (8, 3 * TILE), 0)

    def combine(ref, n):
        vals = [ref[k] for k in range(n)]
        top = vals[0][0:1]
        keep = vals[0][3:4]
        for v in vals[1:]:
            top = jnp.maximum(top, v[0:1])
            keep = jnp.maximum(keep, v[3:4])
        tot = jnp.zeros_like(top)
        extra = jnp.zeros_like(top)
        for v in vals:
            f = jnp.exp(v[0:1] - top)
            tot = tot + v[1:2] * f
            extra = extra + v[2:3] * jnp.where(lane3 >= 4 * EDITS, f, 1.0)
        return top, tot, extra, keep

    def pack(a, b, d, e):
        return jnp.where(
            row8 == 0, a, jnp.where(row8 == 1, b, jnp.where(row8 == 2, d, e))
        )

    def exchange(ref, me, n, device):
        first_id = ids(n)
        cps = []
        for j in range(1, n):
            cp = remote(ref.at[me], ref.at[me], first_id + j, device(j))
            cp.start()
            cps.append(cp)
        for cp in cps:
            cp.wait_recv()
        sent.extend(cps)

    st1[g] = stc[...].T[0:8, :]
    exchange(st1, g, 8, lambda j: (z, y * 8 + (g + j) % 8))
    st2[y] = pack(*combine(st1, 8))
    exchange(st2, y, 4, lambda j: dev(z, at(y, j), x, c))
    st3[z] = pack(*combine(st2, 4))
    exchange(st3, z, 4, lambda j: dev(at(z, j), y, x, c))
    top, tot, extra, keep = combine(st3, 4)
    extra = jnp.where(lane3 >= 4 * EDITS, extra / tot, extra)
    str_[0:8, :] = pack(top + jnp.log(tot), extra, keep, keep)
    str_[8:, :] = jnp.zeros((TILE - 8, 3 * TILE), F32)
    stc[...] = str_[...].T

    def col(s, k):
        return stc[s * EDITS : (s + 1) * EDITS, k : k + 1]

    lens = tlen[...]
    inner = jnp.zeros((EDITS, TILE), F32)
    loss = KL_WEIGHT * (col(4, 1) - col(4, 0) + col(3, 0))
    for s in range(4):
        lg = logits(s)
        prob = jnp.exp(lg - col(s, 0))
        if s < TGT:
            hit = (targets[:, s : s + 1] == vocab).astype(F32)
            wt = (s < lens).astype(F32) / lens.astype(F32)
            dg = (prob - hit) * wt
            loss = loss - jnp.where(s < lens, (col(s, 1) - col(s, 0)) * wt, 0.0)
        else:
            dg = KL_WEIGHT * (prob - jnp.exp(logits(4) - col(4, 0)))
        dg = dg.astype(BF16)
        dl[s * EDITS : (s + 1) * EDITS, :] = dg
        part = jnp.sum(dg.astype(F32) * lg, axis=-1, keepdims=True)
        inner = jnp.where(lane == s, part, inner)
    for i in range(2):
        own = jnp.where(row == 2 * dp + i, loss, 0.0)
        loss_out[i : i + 1, :] = jnp.broadcast_to(
            jnp.sum(own, axis=0, keepdims=True), (1, TILE)
        )

    for k in range(16):
        usend[0, k, :, 0:TILE] = inner[4 * k : 4 * k + 4, :]
        usend[1, k, :, 0:TILE] = jnp.zeros((4, TILE), F32)

    p_ids = ids(5)
    x_ids = ids(16 * 5)
    z_ids = ids(8 * 5)

    def cols_of(n):
        return pl.ds(pl.multiple_of(TILE + n * SLICE, TILE), SLICE)

    COL0 = pl.ds(0, TILE)

    def give_half(n, cols):
        return remote(usend.at[1 - c, :, :, cols], precv.at[:, :, cols], p_ids + n, PART)

    def x_copy(n, cols, j):
        yy, xx = at(y, j // 4), at(x, j % 4)
        return remote(
            usend.at[c, yy * 4 + xx, :, cols], xrecv.at[chip, :, cols],
            x_ids + n * 16 + j, dev(z, yy, xx, c),
        )

    def z_copy(n, cols, j):
        to = (u + j) % 8
        return remote(
            zsrc.at[to % 2, :, cols], zrecv.at[u, :, cols],
            z_ids + n * 8 + j, dev(to // 2, y, x, to % 2),
        )

    def loop(lo, hi, body):
        def run(j, carry):
            body(j)
            return carry
        lax.fori_loop(lo, hi, run, 0)

    def spread(n, cols):
        give_half(n, cols).wait_recv()
        both = usend[c, :, :, cols] + precv[:, :, cols]
        usend[c, :, :, cols] = both
        xrecv[chip, :, cols] = usend[c, chip, :, cols]
        loop(1, 16, lambda j: x_copy(n, cols, j).start())

    def plane(n, cols):
        loop(1, 16, lambda j: x_copy(n, cols, j).wait_recv())
        total = xrecv[0, :, cols]
        for k in range(1, 16):
            total = total + xrecv[k, :, cols]
        for k in range(2):
            zsrc[k, :, cols] = total[2 * k : 2 * k + 2, :]
        zrecv[u, :, cols] = zsrc[c, :, cols]
        loop(1, 8, lambda j: z_copy(n, cols, j).start())

    def part(n, sub):
        grad = jnp.dot(dl[...], hv[2 * n + sub], preferred_element_type=F32)
        mix = grad[0:EDITS] * col(0, 2)
        for s in range(1, 4):
            mix = mix + grad[s * EDITS : (s + 1) * EDITS] * col(s, 2)
        for k in range(16):
            usend[sub, k, :, cols_of(n)] = mix[4 * k : 4 * k + 4, :]

    give_half(4, COL0).start()

    def grads(n):
        part(n, 1 - c)
        give_half(n, cols_of(n)).start()
        pl.when(n == 0)(lambda: spread(4, COL0))
        pl.when(n > 0)(lambda: spread(n - 1, cols_of(n - 1)))
        part(n, c)

    loop(0, 4, grads)
    spread(3, cols_of(3))
    plane(4, COL0)
    loop(0, 4, lambda n: plane(n, cols_of(n)))

    loop(1, 8, lambda j: z_copy(4, COL0, j).wait_recv())
    inn = zrecv[0, :, 0:TILE]
    for k in range(1, 8):
        inn = inn + zrecv[k, :, 0:TILE]
    coef = [invs[s] * invs[s] * inn[:, s : s + 1] / D for s in range(4)]
    for n in range(4):
        loop(1, 8, lambda j: z_copy(n, cols_of(n), j).wait_recv())
        for hf in range(2):
            cols = pl.ds((2 * n + hf) * SLICE, SLICE)
            mine = zrecv[hf, :, cols_of(n)]
            for k in range(1, 4):
                mine = mine + zrecv[2 * k + hf, :, cols_of(n)]
            shift = delta[:, cols]
            back = jnp.zeros((2, SLICE), F32)
            for s in range(4):
                back = back + (hidden[:, s, cols].astype(F32) + shift) * coef[s]
            step_out[:, cols] = -STEP_RATE * (gain[:, cols] * mine - back)

    for cp in sent:
        cp.wait_send()
    for ring in [a1, b1, a2] + [b2[k] for k in range(4)]:
        ring.drain()
    for k in range(4):
        for h in range(2):
            pair(k, h).wait_send()
    give_half(4, COL0).wait_send()
    loop(1, 16, lambda j: x_copy(4, COL0, j).wait_send())
    loop(1, 8, lambda j: z_copy(4, COL0, j).wait_send())

    def drain(n):
        give_half(n, cols_of(n)).wait_send()
        loop(1, 16, lambda j: x_copy(n, cols_of(n), j).wait_send())
        loop(1, 8, lambda j: z_copy(n, cols_of(n), j).wait_send())

    loop(0, 4, drain)
    assert count[0] <= SEMS


SEMS = 256


def local(hidden, delta, gain, head, targets, tlen):
    vm = pl.BlockSpec(memory_space=pltpu.VMEM)
    scratch = [
        pltpu.VMEM((8, V, SLICE), BF16),
        pltpu.VMEM((2, 4, 2, 5, 4, 16, HALF), BF16),
        pltpu.VMEM((5 * EDITS, V), F32),
        pltpu.VMEM((4 * EDITS, V), BF16),
        pltpu.VMEM((8, 5, 2, SLICE), BF16),
        pltpu.VMEM((8, 5, 2, SLICE), BF16),
        pltpu.VMEM((5, 16, SLICE), F32),
        pltpu.VMEM((3 * TILE, TILE), F32),
        pltpu.VMEM((TILE, 3 * TILE), F32),
        pltpu.VMEM((8, 8, 3 * TILE), F32),
        pltpu.VMEM((4, 8, 3 * TILE), F32),
        pltpu.VMEM((4, 8, 3 * TILE), F32),
        pltpu.VMEM((2, 16, 4, UCOLS), F32),
        pltpu.VMEM((16, 4, UCOLS), F32),
        pltpu.VMEM((16, 4, UCOLS), F32),
        pltpu.VMEM((2, 2, UCOLS), F32),
        pltpu.VMEM((8, 2, UCOLS), F32),
        pltpu.SemaphoreType.DMA((8,)),
        pltpu.SemaphoreType.DMA((SEMS,)),
        pltpu.SemaphoreType.DMA((SEMS,)),
    ]
    step, loss = pl.pallas_call(
        kernel,
        out_shape=(
            jax.ShapeDtypeStruct((2, D), F32),
            jax.ShapeDtypeStruct((2, TILE), F32),
        ),
        in_specs=[vm, vm, vm, pl.BlockSpec(memory_space=pl.ANY), vm, vm],
        out_specs=(vm, vm),
        scratch_shapes=scratch,
        compiler_params=pltpu.CompilerParams(
            collective_id=0, has_side_effects=True, vmem_limit_bytes=56 * 2**20
        ),
    )(hidden, delta, gain.reshape(1, D), head, targets, tlen.reshape(EDITS, 1))
    return (loss[:, 0], step)


def solution(mesh):
    placed = (P("dp", None, None), P("dp", None), P(), P(("section", "dp"), None), P(), P())
    return jax.shard_map(
        local, mesh=mesh, in_specs=placed, out_specs=(P("dp"), P("dp", None)), check_vma=False
    )
```

time: 341 us -> 86.5 us (0.25)
  waiting for transfers between devices: 150 us -> 0 us
  blocking collectives: 133 us -> 0 us
  Pallas kernels: 0 us -> 80.2 us
  matrix products: 28.3 us -> 0 us
  between operations: 14.2 us -> 0.64 us
  other arithmetic: 10.6 us -> 0 us
    psum x1 -> x0, waiting for transfers between devices: 94.6 us -> none  [local(): lax.psum(jnp.dot(dlogits, head, preferred_element_type=jnp.float32), ('se...]
    pallas_call x0 -> x1, Pallas kernels: none -> 80.2 us  [local(): pl.pallas_call(kernel, out_shape=(jax.ShapeDtypeStruct((2, D), F32), jax....]
    all_gather x2 -> x0, blocking collectives: 70.7 us -> none  [joined(): pieces = jax.tree.map(lambda part: lax.all_gather(part, axis), value)]
    psum x1 -> x0, blocking collectives: 62.6 us -> none  [local(): tgt_sum, kl = lax.psum((tgt_local, kl_local), ('section', 'dp'))]
    all_gather x1 -> x0, waiting for transfers between devices: 55 us -> none  [local(): lax.all_gather(rows, 'dp', axis=0, tiled=True)]
    dot_general x2 -> x0, matrix products: 28.3 us -> none  [the longest x1 15.8 us: local(): lax.dot_general(lax.all_gather(rows, 'dp', axis=0, tiled=True), head, (((...]
    convert_element_type x4 -> x0, other arithmetic: 3.54 us -> none  [the longest x1 1.06 us: local(): normed.astype(jnp.bfloat16)]
  transfers between devices with their start and end apart: 2 -> 0, of which waited for: 2 -> 0; matrix products, arithmetic and copies ran while one was open for 1% -> 0% of each run, Pallas kernels for 0% -> 0%
where the time goes in v2:
time: 86.5 us; the launch traced here: 86.3 us
  Pallas kernels  80.2 us (93%)
  local copies, waits for them, and re-layouts  5.49 us (6%)
    pallas_call x1, Pallas kernels, local(): pl.pallas_call(kernel, out_shape=(jax.ShapeDtypeStruct((2, D), F32), jax....  80.2 us
    unnamed x2, local copies, waits for them, and re-layouts  2.86 us

profile of v2, /device:TPU:1, one launch (start us, length us, event | category | flops | bytes accessed | tf_op | source)
XLA Modules:
  0.0 86.3 jit_solution(9914514629350308397)
XLA Ops:
  0.6 1.4 %copy.10.targets = s32[64,3]{1,0:T(8,128)} copy(s32[64,3]{0,1:T(4,128)} %param.10) | data formatting | bytes 1536 | tf_op args[4]
  2.0 1.3 %copy.11.tlen = s32[64,1]{1,0:T(8,128)} copy(s32[64,1]{0,1:T(1,128)} %bitcast.3) | data formatting | bytes 512 | tf_op jit(solution)/shard_map/reshape | solution.py:547
  3.4 80.2 %shard_map.77 = (f32[2,8192]{1,0:T(2,128)}, f32[2,128]{1,0:T(2,128)}) custom-call(bf16[2,4,8192]{2,1,0:T(4,128)(2,1)} %hidden.1, f32[2,8192]{1,0:T(2,128)} %delta.1, f32[1,8192]{1,0:T(1,128)} %bitcast.2, bf16[1024,8192]{1,0:T(8,128)(2,1)} %head.1, s32[64,3]{1,0:T(8,128)} %copy.10.targets, s32[64,1]{1,0:T(8,128)} %copy.11.tlen), custom_call_target="tpu_custom_call" | custom-call | tf_op jit(solution)/shard_map/pallas_call | solution.py:535
  83.5 1.3 %slice_reduce_fusion = f32[2]{0:T(128)} fusion(f32[2,128]{1,0:T(2,128)} %get-tuple-element.4), kind=kLoop, calls=%fused_computation | loop fusion | bytes 16 | tf_op jit(solution)/shard_map/slice | solution.py:548
  84.8 1.5 %copy.13 = f32[2,8192]{1,0:T(2,128)} copy(f32[2,8192]{1,0:T(2,128)} %get-tuple-element.9) | data formatting | bytes 131072
